TPU v7x, 256 devices: a whole 4x4x8 slice. The times are simulated.
256 devices in a mesh: rows: 8 (over y, core), vecs: 32 (over x, z).
Axes of the slice: x: 4, y: 4, z: 8, core: 2. Of those that a mesh axis runs over, the one named last changes fastest.
Arguments:
- vectors: float32 [4096, 8192], P('rows', 'vecs'), may hold values from -6 to 6
- reflectors: float32 [4, 16, 512, 256], P(None, 'rows', 'vecs'), may hold values from -0.4 to 1, as said below
Outputs:
- transformed: float32 [4096, 8192], P('rows', 'vecs')
Inputs may be any that keep to these rules, and one draw needn't show every extreme that they name: reflectors[t, b] is unit lower trapezoidal: entry (i, j) is 1 where i == j and 0 where i < j.
All inputs are finite; a program needn't handle non-finite values.
Results may differ from a plain program's by a relative error of at most 0.00026.
Values sent between devices are 32-bit elements; how exact they have to be, the bound alone decides.
A program may use at most 128 MiB of HBM per device.

v0:
```python
import jax
import jax.numpy as jnp
from jax import lax
from jax.sharding import PartitionSpec as P


def passed_along(value, axis, steps):
    count = lax.axis_size(axis)
    leading, last = (max(0, -steps), min(count, count - steps))
    return lax.ppermute(value, axis, [(source, source + steps) for source in range(leading, last)])


def invert_upper(matrix):
    size = matrix.shape[-1]
    if size == 1:
        return 1.0 / matrix
    half = size // 2
    upper_left = matrix[:, :half, :half]
    corner = matrix[:, :half, half:]
    lower_right = matrix[:, half:, half:]
    if half * 2 == size:
        count = matrix.shape[0]
        both = invert_upper(jnp.concatenate([upper_left, lower_right], axis=0))
        left_inverse = both[:count]
        right_inverse = both[count:]
    else:
        left_inverse = invert_upper(upper_left)
        right_inverse = invert_upper(lower_right)
    middle = jnp.einsum("bij,bjk->bik", corner, right_inverse, precision=lax.Precision.HIGHEST)
    middle = -jnp.einsum("bij,bjk->bik", left_inverse, middle, precision=lax.Precision.HIGHEST)
    zeros_block = jnp.zeros((matrix.shape[0], size - half, half), matrix.dtype)
    top = jnp.concatenate([left_inverse, middle], axis=2)
    bottom = jnp.concatenate([zeros_block, right_inverse], axis=2)
    return jnp.concatenate([top, bottom], axis=1)


def make_inverses(gram_full):
    diagonal = jnp.diagonal(gram_full, axis1=1, axis2=2)
    identity = jnp.eye(gram_full.shape[-1], dtype=gram_full.dtype)
    factors = jnp.triu(gram_full, 1) + 0.5 * identity * diagonal[:, None, :]
    return invert_upper(factors)


def reflect(window_rows, vblock, inverse):
    products = jnp.einsum("ri,rc->ic", vblock, window_rows, precision=lax.Precision.HIGHEST)
    solved = jnp.dot(inverse, products, precision=lax.Precision.HIGHEST)
    return window_rows - jnp.dot(vblock, solved, precision=lax.Precision.HIGHEST)


def local(vectors, reflectors):
    rows_dev = vectors.shape[0]
    block_count = reflectors.shape[1]
    width = reflectors.shape[3]
    topmost = lax.axis_index("rows") == 0
    lowest = lax.axis_index("rows") == lax.axis_size("rows") - 1
    tail_rows = jnp.zeros((width, vectors.shape[1]), jnp.float32)
    gathered = lax.all_gather(reflectors, "vecs", axis=2, tiled=True)
    current = vectors
    for moment in range(reflectors.shape[0]):
        blocks = gathered[moment]
        gram_full = jnp.einsum("bri,brj->bij", blocks, blocks, precision=lax.Precision.HIGHEST)
        inverses = make_inverses(gram_full)
        current = current.at[: 2 * width].set(reflect(current[: 2 * width], blocks[0], inverses[0]))
        shifted = passed_along(current[:width], "rows", -1)
        beneath = jnp.where(lowest, tail_rows, shifted)
        for column in range(1, block_count - 1):
            start = column * width
            current = current.at[start : start + 2 * width].set(
                reflect(current[start : start + 2 * width], blocks[column], inverses[column])
            )
        joined = jnp.concatenate([current[rows_dev - width :], beneath], axis=0)
        joined = reflect(joined, blocks[block_count - 1], inverses[block_count - 1])
        tail_rows = joined[width:]
        returned = passed_along(joined[width:], "rows", 1)
        current = jnp.concatenate(
            [
                jnp.where(topmost, current[:width], returned),
                current[width : rows_dev - width],
                joined[:width],
            ],
            axis=0,
        )
    return current


def solution(mesh):
    placed = (P("rows", "vecs"), P(None, "rows", "vecs", None))
    return jax.shard_map(
        local, mesh=mesh, in_specs=placed, out_specs=P("rows", "vecs"), check_vma=False
    )
```

profile of v0, /device:TPU:16, one launch (start us, length us, event | category | flops | bytes accessed | tf_op | source)
XLA Modules:
  0.0 328.1 jit_solution(1579442743634784722)
XLA Ops:
  8.7 85.7 %all-gather.2.cloned.1.call-done = f32[4,2,512,256]{3,2,1,0:T(8,128)} async-done(((f32[4,2,16,256]{3,2,1,0:T(8,128)}), f32[4,2,512,256]{3,2,1,0:T(8,128)}) %all-gather.2.cloned.1.call-update) | async-done | bytes 4194320 | tf_op jit(solution)/shard_map/all_gather | solution.py:57
  94.5 3.4 %fusion.11 = f32[2,256,256]{2,1,0:T(8,128)S(1)} fusion(f32[4,2,512,256]{3,2,1,0:T(8,128)} %all-gather.2.cloned.1.call-done), kind=kOutput, calls=%fused_computation.55 | convolution fusion | flops 805306368 | bytes 1572864 | tf_op jit(solution)/shard_map/bri,brj->bij/dot_general | solution.py:61
  97.9 17.0 %copy.201 = f32[2,256,256]{0,2,1:T(8,128)} copy(f32[2,256,256]{2,1,0:T(8,128)S(1)} %fusion.11) | data formatting | bytes 1048576 | tf_op jit(solution)/shard_map/bri,brj->bij/dot_general | solution.py:61
  114.9 2.3 gather_fusion
  117.3 3.6 %fusion.10 = f32[2,256,256]{2,1,0:T(8,128)S(1)} fusion(f32[4,2,512,256]{3,2,1,0:T(8,128)} %all-gather.2.cloned.1.call-done), kind=kOutput, calls=%fused_computation.53 | convolution fusion | flops 805306368 | bytes 1572864 | tf_op jit(solution)/shard_map/bri,brj->bij/dot_general | solution.py:61
  120.9 16.8 %copy.213 = f32[2,256,256]{0,2,1:T(8,128)} copy(f32[2,256,256]{2,1,0:T(8,128)S(1)} %fusion.10) | data formatting | bytes 1048576 | tf_op jit(solution)/shard_map/bri,brj->bij/dot_general | solution.py:61
  137.7 2.3 gather_fusion.1
  140.1 3.4 %fusion.9 = f32[2,256,256]{2,1,0:T(8,128)S(1)} fusion(f32[4,2,512,256]{3,2,1,0:T(8,128)} %all-gather.2.cloned.1.call-done), kind=kOutput, calls=%fused_computation.51 | convolution fusion | flops 805306368 | bytes 1572864 | tf_op jit(solution)/shard_map/bri,brj->bij/dot_general | solution.py:61
  143.5 16.8 %copy.224 = f32[2,256,256]{0,2,1:T(8,128)} copy(f32[2,256,256]{2,1,0:T(8,128)S(1)} %fusion.9) | data formatting | bytes 1048576 | tf_op jit(solution)/shard_map/bri,brj->bij/dot_general | solution.py:61
  160.3 2.3 gather_fusion.2
  162.7 3.4 %fusion.8 = f32[2,256,256]{2,1,0:T(8,128)S(1)} fusion(f32[4,2,512,256]{3,2,1,0:T(8,128)} %all-gather.2.cloned.1.call-done), kind=kOutput, calls=%fused_computation.49 | convolution fusion | flops 805306368 | bytes 1572864 | tf_op jit(solution)/shard_map/bri,brj->bij/dot_general | solution.py:61
  166.1 17.2 %copy.235 = f32[2,256,256]{0,2,1:T(8,128)} copy(f32[2,256,256]{2,1,0:T(8,128)S(1)} %fusion.8) | data formatting | bytes 1048576 | tf_op jit(solution)/shard_map/bri,brj->bij/dot_general | solution.py:61
  183.3 2.3 gather_fusion.3
  252.0 3.5 %collective-permute-done = f32[256,256]{0,1:T(8,128)S(1)} collective-permute-done((f32[256,256]{0,1:T(8,128)S(1)}, f32[256,256]{0,1:T(8,128)S(1)}, u32[]{:S(2)}, u32[]{:S(2)}) %collective-permute-start) | collective-permute-done | bytes 262176 | tf_op jit(solution)/shard_map/ppermute | solution.py:10
  257.7 3.4 %collective-permute-start.1 = (f32[256,256]{0,1:T(8,128)S(1)}, f32[256,256]{0,1:T(8,128)S(1)}, u32[]{:S(2)}, u32[]{:S(2)}) collective-permute-start(f32[256,256]{0,1:T(8,128)S(1)} %get-tuple-element.103), channel_id=1, source_target_pairs={{0,32},{32,64},{64,96},{96,128},{128,160},{160,192},{192,224},{1,3... | collective-permute-start | bytes 786440 | tf_op jit(solution)/shard_map/ppermute | solution.py:10
  261.5 4.1 %collective-permute-done.1 = f32[256,256]{0,1:T(8,128)S(1)} collective-permute-done((f32[256,256]{0,1:T(8,128)S(1)}, f32[256,256]{0,1:T(8,128)S(1)}, u32[]{:S(2)}, u32[]{:S(2)}) %collective-permute-start.1) | collective-permute-done | bytes 262176 | tf_op jit(solution)/shard_map/ppermute | solution.py:10
  275.9 3.4 %collective-permute-start.3 = (f32[256,256]{0,1:T(8,128)S(1)}, f32[256,256]{0,1:T(8,128)S(1)}, u32[]{:S(2)}, u32[]{:S(2)}) collective-permute-start(f32[256,256]{0,1:T(8,128)S(1)} %get-tuple-element.97), channel_id=1, source_target_pairs={{0,32},{32,64},{64,96},{96,128},{128,160},{160,192},{192,224},{1,3... | collective-permute-start | bytes 786440 | tf_op jit(solution)/shard_map/ppermute | solution.py:10
  279.5 4.3 %collective-permute-done.3 = f32[256,256]{0,1:T(8,128)S(1)} collective-permute-done((f32[256,256]{0,1:T(8,128)S(1)}, f32[256,256]{0,1:T(8,128)S(1)}, u32[]{:S(2)}, u32[]{:S(2)}) %collective-permute-start.3) | collective-permute-done | bytes 262176 | tf_op jit(solution)/shard_map/ppermute | solution.py:10
  288.6 3.1 collective-permute-done.4
  293.9 3.4 %collective-permute-start.5 = (f32[256,256]{0,1:T(8,128)S(1)}, f32[256,256]{0,1:T(8,128)S(1)}, u32[]{:S(2)}, u32[]{:S(2)}) collective-permute-start(f32[256,256]{0,1:T(8,128)S(1)} %get-tuple-element.91), channel_id=1, source_target_pairs={{0,32},{32,64},{64,96},{96,128},{128,160},{160,192},{192,224},{1,3... | collective-permute-start | bytes 786440 | tf_op jit(solution)/shard_map/ppermute | solution.py:10
  297.3 4.4 %collective-permute-done.5 = f32[256,256]{0,1:T(8,128)S(1)} collective-permute-done((f32[256,256]{0,1:T(8,128)S(1)}, f32[256,256]{0,1:T(8,128)S(1)}, u32[]{:S(2)}, u32[]{:S(2)}) %collective-permute-start.5) | collective-permute-done | bytes 262176 | tf_op jit(solution)/shard_map/ppermute | solution.py:10
  305.8 3.9 %collective-permute-done.6 = f32[256,256]{0,1:T(8,128)S(1)} collective-permute-done((f32[256,256]{0,1:T(8,128)S(1)}, f32[256,256]{0,1:T(8,128)S(1)}, u32[]{:S(2)}, u32[]{:S(2)}) %collective-permute-start.6) | collective-permute-done | bytes 262176 | tf_op jit(solution)/shard_map/ppermute | solution.py:10
  311.9 3.4 %collective-permute-start.7 = (f32[256,256]{0,1:T(8,128)S(1)}, f32[256,256]{0,1:T(8,128)S(1)}, u32[]{:S(2)}, u32[]{:S(2)}) collective-permute-start(f32[256,256]{0,1:T(8,128)S(1)} %get-tuple-element.85), channel_id=1, source_target_pairs={{0,32},{32,64},{64,96},{96,128},{128,160},{160,192},{192,224},{1,3... | collective-permute-start | bytes 786440 | tf_op jit(solution)/shard_map/ppermute | solution.py:10
  315.2 4.5 %collective-permute-done.7 = f32[256,256]{0,1:T(8,128)S(1)} collective-permute-done((f32[256,256]{0,1:T(8,128)S(1)}, f32[256,256]{0,1:T(8,128)S(1)}, u32[]{:S(2)}, u32[]{:S(2)}) %collective-permute-start.7) | collective-permute-done | bytes 262176 | tf_op jit(solution)/shard_map/ppermute | solution.py:10
  (283 shorter events, 94.9 us)
Async XLA Ops:
  6.5 87.9 %all-gather.2.cloned.1.call-start = ((), (), s32[]{:S(2)}) async-start(), calls=%async_computation | async-start | bytes 4325376 | tf_op jit(solution)/shard_map/all_gather | solution.py:57
  202.9 3.9 %copy-start.3 = (f32[2,256,256]{2,1,0:T(8,128)S(1)}, f32[2,256,256]{2,1,0:T(8,128)}, u32[]{:S(2)}) copy-start(f32[2,256,256]{2,1,0:T(8,128)} %get-tuple-element.112) | copy-start | bytes 1572868
  202.9 3.9 %copy-start.4 = (f32[2,256,256]{2,1,0:T(8,128)S(1)}, f32[2,256,256]{2,1,0:T(8,128)}, u32[]{:S(2)}) copy-start(f32[2,256,256]{2,1,0:T(8,128)} %get-tuple-element.110) | copy-start | bytes 1572868
  207.6 13.2 %copy-start.12 = (f32[2,128,128]{2,1,0:T(8,128)}, f32[2,128,128]{2,1,0:T(8,128)S(1)}, u32[]{:S(2)}) copy-start(f32[2,128,128]{2,1,0:T(8,128)S(1)} %get-tuple-element.102) | copy-start | bytes 393220
  208.3 12.4 %copy-start.5 = (f32[16,16,16]{2,1,0:T(8,128)}, f32[16,16,16]{2,1,0:T(8,128)S(1)}, u32[]{:S(2)}) copy-start(f32[16,16,16]{2,1,0:T(8,128)S(1)} %get-tuple-element.168) | copy-start | bytes 49156
  227.2 4.2 %copy-start.7 = (f32[2,128,128]{2,1,0:T(8,128)S(1)}, f32[2,128,128]{2,1,0:T(8,128)}, u32[]{:S(2)}) copy-start(f32[2,128,128]{2,1,0:T(8,128)} %get-tuple-element.215) | copy-start | bytes 393220
  227.2 4.2 %copy-start.8 = (f32[2,128,128]{2,1,0:T(8,128)S(1)}, f32[2,128,128]{2,1,0:T(8,128)}, u32[]{:S(2)}) copy-start(f32[2,128,128]{2,1,0:T(8,128)} %get-tuple-element.216) | copy-start | bytes 393220
  244.1 3.0 copy-start
  245.6 6.1 %copy-start.20 = (f32[2,128,128]{2,1,0:T(8,128)S(1)}, f32[2,128,128]{2,1,0:T(8,128)}, u32[]{:S(2)}) copy-start(f32[2,128,128]{2,1,0:T(8,128)} %get-tuple-element.153) | copy-start | bytes 393220
  245.6 6.1 %copy-start.21 = (f32[2,128,128]{2,1,0:T(8,128)S(1)}, f32[2,128,128]{2,1,0:T(8,128)}, u32[]{:S(2)}) copy-start(f32[2,128,128]{2,1,0:T(8,128)} %get-tuple-element.154) | copy-start | bytes 393220
  246.2 5.6 %copy-start.24 = (f32[4,64,64]{2,1,0:T(8,128)S(1)}, f32[4,64,64]{2,1,0:T(8,128)}, u32[]{:S(2)}) copy-start(f32[4,64,64]{2,1,0:T(8,128)} %fusion.73) | copy-start | bytes 196612
  249.5 11.5 %copy-start.18 = (f32[4,64,64]{2,1,0:T(8,128)S(1)}, f32[4,64,64]{2,1,0:T(8,128)}, u32[]{:S(2)}) copy-start(f32[4,64,64]{2,1,0:T(8,128)} %get-tuple-element.135) | copy-start | bytes 196612
  249.6 11.5 %copy-start.19 = (f32[4,64,64]{2,1,0:T(8,128)S(1)}, f32[4,64,64]{2,1,0:T(8,128)}, u32[]{:S(2)}) copy-start(f32[4,64,64]{2,1,0:T(8,128)} %get-tuple-element.136) | copy-start | bytes 196612
  249.6 11.7 %copy-start.23 = (f32[4,64,64]{2,1,0:T(8,128)S(1)}, f32[4,64,64]{2,1,0:T(8,128)}, u32[]{:S(2)}) copy-start(f32[4,64,64]{2,1,0:T(8,128)} %fusion.63) | copy-start | bytes 196612
  249.6 5.9 %collective-permute-start = (f32[256,256]{0,1:T(8,128)S(1)}, f32[256,256]{0,1:T(8,128)S(1)}, u32[]{:S(2)}, u32[]{:S(2)}) collective-permute-start(f32[256,256]{0,1:T(8,128)S(1)} %get-tuple-element.106), channel_id=1, source_target_pairs={{32,0},{64,32},{96,64},{128,96},{160,128},{192,160},{224,192},{33,... | collective-permute-start | bytes 786440 | tf_op jit(solution)/shard_map/ppermute | solution.py:10
  257.7 7.9 %collective-permute-start.1 = (f32[256,256]{0,1:T(8,128)S(1)}, f32[256,256]{0,1:T(8,128)S(1)}, u32[]{:S(2)}, u32[]{:S(2)}) collective-permute-start(f32[256,256]{0,1:T(8,128)S(1)} %get-tuple-element.103), channel_id=1, source_target_pairs={{0,32},{32,64},{64,96},{96,128},{128,160},{160,192},{192,224},{1,3... | collective-permute-start | bytes 786440 | tf_op jit(solution)/shard_map/ppermute | solution.py:10
  267.7 11.6 %copy-start.16 = (f32[4,64,64]{2,1,0:T(8,128)S(1)}, f32[4,64,64]{2,1,0:T(8,128)}, u32[]{:S(2)}) copy-start(f32[4,64,64]{2,1,0:T(8,128)} %get-tuple-element.115) | copy-start | bytes 196612
  267.7 11.6 %copy-start.17 = (f32[4,64,64]{2,1,0:T(8,128)S(1)}, f32[4,64,64]{2,1,0:T(8,128)}, u32[]{:S(2)}) copy-start(f32[4,64,64]{2,1,0:T(8,128)} %get-tuple-element.116) | copy-start | bytes 196612
  267.8 5.9 %collective-permute-start.2 = (f32[256,256]{0,1:T(8,128)S(1)}, f32[256,256]{0,1:T(8,128)S(1)}, u32[]{:S(2)}, u32[]{:S(2)}) collective-permute-start(f32[256,256]{0,1:T(8,128)S(1)} %get-tuple-element.100), channel_id=1, source_target_pairs={{32,0},{64,32},{96,64},{128,96},{160,128},{192,160},{224,192},{33,... | collective-permute-start | bytes 786440 | tf_op jit(solution)/shard_map/ppermute | solution.py:10
  275.9 7.9 %collective-permute-start.3 = (f32[256,256]{0,1:T(8,128)S(1)}, f32[256,256]{0,1:T(8,128)S(1)}, u32[]{:S(2)}, u32[]{:S(2)}) collective-permute-start(f32[256,256]{0,1:T(8,128)S(1)} %get-tuple-element.97), channel_id=1, source_target_pairs={{0,32},{32,64},{64,96},{96,128},{128,160},{160,192},{192,224},{1,3... | collective-permute-start | bytes 786440 | tf_op jit(solution)/shard_map/ppermute | solution.py:10
  285.9 5.8 %collective-permute-start.4 = (f32[256,256]{0,1:T(8,128)S(1)}, f32[256,256]{0,1:T(8,128)S(1)}, u32[]{:S(2)}, u32[]{:S(2)}) collective-permute-start(f32[256,256]{0,1:T(8,128)S(1)} %get-tuple-element.94), channel_id=1, source_target_pairs={{32,0},{64,32},{96,64},{128,96},{160,128},{192,160},{224,192},{33,... | collective-permute-start | bytes 786440 | tf_op jit(solution)/shard_map/ppermute | solution.py:10
  293.9 7.9 %collective-permute-start.5 = (f32[256,256]{0,1:T(8,128)S(1)}, f32[256,256]{0,1:T(8,128)S(1)}, u32[]{:S(2)}, u32[]{:S(2)}) collective-permute-start(f32[256,256]{0,1:T(8,128)S(1)} %get-tuple-element.91), channel_id=1, source_target_pairs={{0,32},{32,64},{64,96},{96,128},{128,160},{160,192},{192,224},{1,3... | collective-permute-start | bytes 786440 | tf_op jit(solution)/shard_map/ppermute | solution.py:10
  303.9 5.8 %collective-permute-start.6 = (f32[256,256]{0,1:T(8,128)S(1)}, f32[256,256]{0,1:T(8,128)S(1)}, u32[]{:S(2)}, u32[]{:S(2)}) collective-permute-start(f32[256,256]{0,1:T(8,128)S(1)} %get-tuple-element.88), channel_id=1, source_target_pairs={{32,0},{64,32},{96,64},{128,96},{160,128},{192,160},{224,192},{33,... | collective-permute-start | bytes 786440 | tf_op jit(solution)/shard_map/ppermute | solution.py:10
  311.9 7.9 %collective-permute-start.7 = (f32[256,256]{0,1:T(8,128)S(1)}, f32[256,256]{0,1:T(8,128)S(1)}, u32[]{:S(2)}, u32[]{:S(2)}) collective-permute-start(f32[256,256]{0,1:T(8,128)S(1)} %get-tuple-element.85), channel_id=1, source_target_pairs={{0,32},{32,64},{64,96},{96,128},{128,160},{160,192},{192,224},{1,3... | collective-permute-start | bytes 786440 | tf_op jit(solution)/shard_map/ppermute | solution.py:10
  (10 other events, 19.7 us)
Sparse Core Ops, SparseCore 0:
  9.9 84.4 all-gather.1
where the time goes:
time: 332 us; the launch traced here: 328 us
  waiting for transfers between devices  116 us (35%)
  local copies, waits for them, and re-layouts  95.8 us (29%)
  matrix products  63.9 us (19%)
  starting transfers between devices  21.7 us (7%)
  between operations  15.4 us (5%)
  other arithmetic  15.2 us (5%)
    all_gather x1, waiting for transfers between devices, local(): gathered = lax.all_gather(reflectors, 'vecs', axis=2, tiled=True)  85.7 us
    dot_general x4, local copies, waits for them, and re-layouts, local(): jnp.einsum('bri,brj->bij', blocks, blocks, precision=lax.Precision.HIGHEST)  67.8 us
    ppermute x8, waiting for transfers between devices, passed_along(): lax.ppermute(value, axis, [(source, source + steps) for source in range(l...  29.6 us
    ppermute x8, starting transfers between devices, passed_along(): lax.ppermute(value, axis, [(source, source + steps) for source in range(l...  21.7 us
    dot_general x28, matrix products, invert_upper(): jnp.einsum('bij,bjk->bik', corner, right_inverse, precision=lax.Precision...  19.7 us
    dot_general x4, matrix products, local(): jnp.einsum('bri,brj->bij', blocks, blocks, precision=lax.Precision.HIGHEST)  13.9 us
    dot_general x28, matrix products, invert_upper(): jnp.einsum('bij,bjk->bik', left_inverse, middle, precision=lax.Precision....  13.4 us
    gather x8, local copies, waits for them, and re-layouts, make_inverses(): diagonal = jnp.diagonal(gram_full, axis1=1, axis2=2)  9.53 us
  transfers between devices with their start and end apart: 9, of which 9 were waited for; matrix products, arithmetic and copies ran while one was open for 1% of the time, Pallas kernels for 0%

commit v1 on v0

v1 whole, which is shorter than its diff:
```python
import jax
import jax.numpy as jnp
from jax import lax
from jax.experimental import pallas as pl
from jax.experimental.pallas import tpu as pltpu
from jax.sharding import PartitionSpec as P

F32, BF16 = jnp.float32, jnp.bfloat16
MESH = pl.DeviceIdType.MESH
STEPS, UNITS = 4, 8
W, C = 256, 128
NX, NZ = 4, 8
ROWS = 8


def split(value):
    high = value.astype(BF16)
    return high, (value - high.astype(F32)).astype(BF16)


def dot(a, b):
    return jnp.dot(a, b, preferred_element_type=F32)


def product(a, b):
    return dot(a[0], b[0]) + (dot(a[0], b[1]) + dot(a[1], b[0]))


def base_inverse(gram, x, upper, eye):
    diagonal = jnp.where(eye, gram, 0.0)
    along = 2.0 / jnp.sum(diagonal, axis=0, keepdims=True)
    down = 2.0 / jnp.sum(diagonal, axis=1, keepdims=True)
    strict = jnp.where(upper, gram, 0.0)
    return strict, jnp.where(eye, along, jnp.where(x == 1, -strict * along * down, 0.0))


def double(stricts, inverses, x, half):
    mask = (x >= half) & (x < 2 * half)
    corners = [split(jnp.where(mask, s, 0.0)) for s in stricts]
    pairs = [split(m) for m in inverses]
    middles = [split(product(b, m)) for b, m in zip(corners, pairs)]
    return [m - product(p, q) for m, p, q in zip(inverses, pairs, middles)]


def kernel(
    vec, refl, out,
    G, VH, VL, TH, TL, ZH, ZL, UB, MB, RET, BEN, UPO, DNO, XB,
    lsem, osem, xs, xr, zs, zr, us, ur, ds, dr,
):
    row = lax.axis_index("rows")
    v = lax.axis_index("vecs")
    x, z = v // NZ, lax.rem(v, NZ)

    def at_x(rel):
        return {"vecs": lax.rem(x + rel, NX) * NZ + z}

    def at_z(d):
        return {"vecs": x * NZ + lax.rem(z + NZ + d, NZ)}

    def local(i):
        if i < 2:
            return pltpu.make_async_copy(
                refl.at[:, :, pl.ds((1 - i) * C, C)], G.at[:, 2 * x + i, z], lsem.at[i]
            )
        half, c = (i - 2) // 2, (i - 2) % 2
        source = vec.at[pl.ds(half * W, W), pl.ds(c * C, C)]
        return pltpu.make_async_copy(source, XB.at[c] if half else RET.at[0, c], lsem.at[i])

    for i in range(6):
        local(i).start()

    barrier = pltpu.get_barrier_semaphore()
    for rel in (1, 2, 3):
        pl.semaphore_signal(barrier, inc=1, device_id=at_x(rel), device_id_type=MESH)
    for d in (1, -1):
        pl.semaphore_signal(barrier, inc=1, device_id=at_z(d), device_id_type=MESH)
        pl.semaphore_signal(
            barrier, inc=1, device_id={"rows": lax.rem(row + ROWS + d, ROWS)}, device_id_type=MESH
        )
    for i in range(6):
        local(i).wait()
    pl.semaphore_wait(barrier, 7)

    def xcopy(u, rel, source):
        slot = G.at[u, pl.ds(2 * source, 2), z]
        return pltpu.make_async_remote_copy(
            slot, slot, xs.at[u, rel - 1], xr.at[u, rel - 1], device_id=at_x(rel), device_id_type=MESH
        )

    def zcopy(u, d, k, source):
        slot = G.at[u, pl.ds(1, 7), source]
        way = 0 if d == 1 else 1
        return pltpu.make_async_remote_copy(
            slot, slot, zs.at[u, way, k - 1], zr.at[u, way, k - 1], device_id=at_z(d), device_id_type=MESH
        )

    def zsend(u, d, k):
        return zcopy(u, d, k, lax.rem(z + NZ - d * (k - 1), NZ))

    def zrecv(u, d, k):
        return zcopy(u, d, k, lax.rem(z + NZ - d * k, NZ))

    def hops(parity, d):
        return 4 if (d == 1) == (parity == 0) else 3

    def ready(u):
        for rel in (1, 2, 3):
            xcopy(u, rel, lax.rem(x + NX - rel, NX)).wait_recv()

    def arrive(u, parity, k):
        for d in (1, -1):
            if k == 0:
                zsend(u, d, 1).start()
            elif k <= hops(parity, d):
                zrecv(u, d, k).wait_recv()
                if k < hops(parity, d):
                    zsend(u, d, k + 1).start()

    for u in range(UNITS):
        for rel in (1, 3, 2):
            xcopy(u, rel, x).start()

    def wave(w, parity):
        for k in (4, 3, 2, 1, 0):
            u = w - k
            if isinstance(w, int):
                if 0 <= u < UNITS:
                    if k == 0:
                        ready(u)
                    arrive(u, u % 2, k)
            else:

                @pl.when(u < UNITS)
                def _(u=u, k=k):
                    if k == 0:
                        ready(u)
                    arrive(u, (parity + k) % 2, k)

    for w in range(4):
        wave(w, None)

    ri = lax.broadcasted_iota(jnp.int32, (W, W), 0)
    ci = lax.broadcasted_iota(jnp.int32, (W, W), 1)

    def prepare_first(t):
        stricts, inverses = [], []
        xor, upper, eye = ri ^ ci, ci > ri, ri == ci
        for j in range(2):
            u = 2 * t + j
            left = jnp.concatenate([G[u, 2 * i + 1].reshape(C, C) for i in range(NX)], axis=0)
            right = jnp.concatenate(
                [jnp.zeros((C, C), F32)] + [G[u, 2 * i].reshape(C, C) for i in range(1, NX)], axis=0
            )
            vh, vl = split(jnp.concatenate([left, right], axis=1))
            th, tl = vh.T, vl.T
            VH[u], VL[u] = vh, vl
            TH[j], TL[j] = th, tl
            strict, inverse = base_inverse(product((th, tl), (vh, vl)), xor, upper, eye)
            stricts.append(strict)
            inverses.append(inverse)
        for half in (2, 4, 8):
            inverses = double(stricts, inverses, xor, half)
        for j in range(2):
            UB[j], MB[j] = stricts[j], inverses[j]

    def prepare_second(t):
        stricts, inverses = [UB[0], UB[1]], [MB[0], MB[1]]
        for half in (16, 32, 64, 128):
            inverses = double(stricts, inverses, ri ^ ci, half)
        for j in range(2):
            zh, zl = split(product(split(inverses[j]), (TH[j], TL[j])))
            ZH[2 * t + j], ZL[2 * t + j] = zh, zl

    def up(t, c):
        return pltpu.make_async_remote_copy(
            UPO.at[t, c], BEN.at[t, c], us.at[t, c], ur.at[t, c],
            device_id={"rows": lax.rem(row + ROWS - 1, ROWS)}, device_id_type=MESH,
        )

    def down(t, c):
        return pltpu.make_async_remote_copy(
            DNO.at[t, c], RET.at[t + 1, c], ds.at[t, c], dr.at[t, c],
            device_id={"rows": lax.rem(row + 1, ROWS)}, device_id_type=MESH,
        )

    def solved_of(u, top, bottom):
        (th, tl), (bh, bl) = split(top), split(bottom)
        rh = jnp.concatenate([th, bh], axis=0)
        rl = jnp.concatenate([tl, bl], axis=0)
        wide = dot(ZH[u], jnp.concatenate([rh, rl], axis=1))
        return split(wide[:, :C] + (wide[:, C:] + dot(ZL[u], rh)))

    def change(u, start, solved):
        wide = dot(VH[u, start : start + W], jnp.concatenate(solved, axis=1))
        return wide[:, :C] + (wide[:, C:] + dot(VL[u, start : start + W], solved[0]))

    def even(t):
        u = 2 * t
        for c in range(2):

            @pl.when((row > 0) & (t > 0))
            def _():
                down(t - 1, c).wait_recv()

            top, bottom = RET[t, c], XB[c]
            solved = solved_of(u, top, bottom)
            top = top - change(u, 0, solved)

            @pl.when(row > 0)
            def _():
                UPO[t, c] = top
                up(t, c).start()

            @pl.when(row == 0)
            def _():
                RET[t + 1, c] = top

            XB[c] = bottom - change(u, W, solved)

    def odd(t):
        u = 2 * t + 1
        for c in range(2):

            @pl.when(row < ROWS - 1)
            def _():
                up(t, c).wait_recv()

            top, bottom = XB[c], BEN[t, c]
            solved = solved_of(u, top, bottom)
            bottom = bottom - change(u, W, solved)

            @pl.when(row < ROWS - 1)
            def _():
                DNO[t, c] = bottom
                down(t, c).start()

            @pl.when(row == ROWS - 1)
            def _():
                BEN[t + 1, c] = bottom

            XB[c] = top - change(u, 0, solved)

    @pl.when(row == ROWS - 1)
    def _():
        BEN[0] = jnp.zeros((2, W, C), F32)

    def tick(t, carry):
        pl.when(t > 0)(lambda: even(t - 1))

        @pl.when(t < STEPS)
        def _():
            wave(2 * t + 4, 0)
            wave(2 * t + 5, 1)
            prepare_first(t)

        pl.when(t > 0)(lambda: odd(t - 1))
        pl.when(t < STEPS)(lambda: prepare_second(t))
        return carry

    lax.fori_loop(0, STEPS + 1, tick, 0)

    def result(half, c):
        target = out.at[pl.ds(half * W, W), pl.ds(c * C, C)]
        return pltpu.make_async_copy(XB.at[c] if half else RET.at[STEPS, c], target, osem.at[half, c])

    for c in range(2):
        result(1, c).start()
    for c in range(2):

        @pl.when(row > 0)
        def _():
            down(STEPS - 1, c).wait_recv()

        result(0, c).start()

    def finish(u, carry):
        for rel in (1, 2, 3):
            xcopy(u, rel, x).wait_send()
        for d in (1, -1):
            for k in range(1, 4):
                zsend(u, d, k).wait_send()
        return carry

    lax.fori_loop(0, UNITS, finish, 0)

    def finish_pair(t, carry):
        zsend(2 * t, 1, 4).wait_send()
        zsend(2 * t + 1, -1, 4).wait_send()
        for c in range(2):
            pl.when(row > 0)(lambda: up(t, c).wait_send())
            pl.when(row < ROWS - 1)(lambda: down(t, c).wait_send())
        return carry

    lax.fori_loop(0, STEPS, finish_pair, 0)
    for half in range(2):
        for c in range(2):
            result(half, c).wait()


def local(vectors, reflectors):
    sem = pltpu.SemaphoreType.DMA
    anywhere = pl.BlockSpec(memory_space=pl.ANY)
    return pl.pallas_call(
        kernel,
        out_shape=jax.ShapeDtypeStruct(vectors.shape, F32),
        in_specs=[anywhere, anywhere],
        out_specs=anywhere,
        scratch_shapes=[
            pltpu.VMEM((UNITS, 2 * NX, NZ, 16, C), F32),
            pltpu.VMEM((UNITS, 2 * W, W), BF16),
            pltpu.VMEM((UNITS, 2 * W, W), BF16),
            pltpu.VMEM((2, W, 2 * W), BF16),
            pltpu.VMEM((2, W, 2 * W), BF16),
            pltpu.VMEM((UNITS, W, 2 * W), BF16),
            pltpu.VMEM((UNITS, W, 2 * W), BF16),
            pltpu.VMEM((2, W, W), F32),
            pltpu.VMEM((2, W, W), F32),
            pltpu.VMEM((STEPS + 1, 2, W, C), F32),
            pltpu.VMEM((STEPS + 1, 2, W, C), F32),
            pltpu.VMEM((STEPS, 2, W, C), F32),
            pltpu.VMEM((STEPS, 2, W, C), F32),
            pltpu.VMEM((2, W, C), F32),
            sem((6,)),
            sem((2, 2)),
            sem((UNITS, 3)),
            sem((UNITS, 3)),
            sem((UNITS, 2, 4)),
            sem((UNITS, 2, 4)),
            sem((STEPS, 2)),
            sem((STEPS, 2)),
            sem((STEPS, 2)),
            sem((STEPS, 2)),
        ],
        compiler_params=pltpu.CompilerParams(
            collective_id=0, has_side_effects=True, vmem_limit_bytes=56 * 2**20
        ),
    )(vectors, reflectors.reshape(UNITS, 16, W))


def solution(mesh):
    placed = (P("rows", "vecs"), P(None, "rows", "vecs", None))
    return jax.shard_map(
        local, mesh=mesh, in_specs=placed, out_specs=P("rows", "vecs"), check_vma=False
    )
```

time: 332 us -> 95.7 us (0.29); the launches traced: 328 us -> 95.6 us
  waiting for transfers between devices: 116 us -> 0 us
  local copies, waits for them, and re-layouts: 95.8 us -> 1.87 us
  Pallas kernels: 0 us -> 93.7 us
  matrix products: 63.9 us -> 0 us
  starting transfers between devices: 21.7 us -> 0 us
  between operations: 15.4 us -> 0.01 us
  other arithmetic: 15.2 us -> 0 us
    pallas_call x0 -> x1, Pallas kernels: none -> 93.7 us  [local(): pl.pallas_call(kernel, out_shape=jax.ShapeDtypeStruct(vectors.shape, F32)...]
    all_gather x1 -> x0, waiting for transfers between devices: 85.7 us -> none  [local(): gathered = lax.all_gather(reflectors, 'vecs', axis=2, tiled=True)]
    dot_general x4 -> x0, local copies, waits for them, and re-layouts: 67.8 us -> none  [local(): jnp.einsum('bri,brj->bij', blocks, blocks, precision=lax.Precision.HIGHEST)]
    dot_general x84 -> x0, matrix products: 63.9 us -> none  [the longest x28 19.7 us: invert_upper(): jnp.einsum('bij,bjk->bik', corner, right_inverse, precision=lax.Precision...]
    ppermute x8 -> x0, waiting for transfers between devices: 29.6 us -> none  [passed_along(): lax.ppermute(value, axis, [(source, source + steps) for source in range(l...]
    ppermute x8 -> x0, starting transfers between devices: 21.7 us -> none  [passed_along(): lax.ppermute(value, axis, [(source, source + steps) for source in range(l...]
    slice x54 -> x0, local copies, waits for them, and re-layouts: 12.1 us -> none  [the longest x8 3.72 us: invert_upper(): corner = matrix[:, :half, half:]]
    concatenate x58 -> x0, other arithmetic: 11.5 us -> none  [the longest x32 6.41 us: invert_upper(): return jnp.concatenate([top, bottom], axis=1)]
  transfers between devices with their start and end apart: 9 -> 0, of which waited for: 9 -> 0; matrix products, arithmetic and copies ran while one was open for 1% -> 0% of each run, Pallas kernels for 0% -> 0%
where the time goes in v1:
time: 95.7 us; the launch traced here: 95.6 us
  Pallas kernels  93.7 us (98%)
  local copies, waits for them, and re-layouts  1.87 us (2%)
    pallas_call x1, Pallas kernels, local(): pl.pallas_call(kernel, out_shape=jax.ShapeDtypeStruct(vectors.shape, F32)...  93.7 us

profile of v1, /device:TPU:16, one launch (start us, length us, event | category | flops | bytes accessed | tf_op | source)
XLA Modules:
  0.0 95.6 jit_solution(14196770641036293686)
XLA Ops:
  0.0 93.7 %shard_map.28 = f32[512,256]{1,0:T(8,128)} custom-call(f32[512,256]{1,0:T(8,128)} %vec.1, f32[8,16,256]{2,1,0:T(8,128)} %bitcast.1), custom_call_target="tpu_custom_call" | custom-call | tf_op jit(solution)/shard_map/pallas_call | solution.py:303
  93.7 1.9 %copy.4 = f32[512,256]{1,0:T(8,128)} copy(f32[512,256]{1,0:T(8,128)} %shard_map.28) | data formatting | bytes 1048576

commit v2 on v1

v2 whole, which is shorter than its diff:
```python
import jax
import jax.numpy as jnp
from jax import lax
from jax.experimental import pallas as pl
from jax.experimental.pallas import tpu as pltpu
from jax.sharding import PartitionSpec as P

F32, BF16 = jnp.float32, jnp.bfloat16
MESH = pl.DeviceIdType.MESH
STEPS, UNITS = 4, 8
W, C = 256, 128
NX, NZ = 4, 8
ROWS = 8


def split(value):
    high = value.astype(BF16)
    return high, (value - high.astype(F32)).astype(BF16)


def dot(a, b):
    return jnp.dot(a, b, preferred_element_type=F32)


def product(a, b):
    return dot(a[0], b[0]) + (dot(a[0], b[1]) + dot(a[1], b[0]))


def narrow_inverse(blocks):
    i = lax.broadcasted_iota(jnp.int32, (16, C), 0)
    lane = lax.broadcasted_iota(jnp.int32, (16, C), 1)
    j = lane % 16
    columns, accs = [], []
    for block in blocks:
        packed = block[:16]
        for k in range(1, C // 16):
            packed = jnp.where(lane // 16 == k, block[16 * k : 16 * k + 16], packed)
        packed = jnp.where(i < j, packed, jnp.where(i == j, 0.5 * packed, 0.0))
        columns.append(
            [jnp.take_along_axis(packed, lane - j + k, axis=1, mode="promise_in_bounds") for k in range(16)]
        )
        accs.append(jnp.where(i == j, 1.0, 0.0))
    for k in range(15, -1, -1):
        for n in range(len(blocks)):
            line = accs[n][k : k + 1] * (1.0 / columns[n][k][k : k + 1])
            accs[n] = jnp.where(i == k, line, accs[n] - columns[n][k] * line)
    ri = lax.broadcasted_iota(jnp.int32, (C, C), 0)
    ci = lax.broadcasted_iota(jnp.int32, (C, C), 1)
    return [jnp.where(ri // 16 == ci // 16, jnp.concatenate([a] * (C // 16), axis=0), 0.0) for a in accs]


def double(grams, inverses, half):
    ri = lax.broadcasted_iota(jnp.int32, (C, C), 0)
    ci = lax.broadcasted_iota(jnp.int32, (C, C), 1)
    mask = (ri ^ ci >= half) & (ri ^ ci < 2 * half) & (ri < ci)
    corners = [split(jnp.where(mask, g, 0.0)) for g in grams]
    pairs = [split(m) for m in inverses]
    middles = [split(product(b, m)) for b, m in zip(corners, pairs)]
    return [m - product(p, q) for m, p, q in zip(inverses, pairs, middles)]


def kernel(
    vec, refl, out,
    G, VH, VL, ZH, ZL, RET, BEN, UPO, DNO, XB,
    lsem, osem, gs, gr, us, ur, ds, dr,
):
    row = lax.axis_index("rows")
    v = lax.axis_index("vecs")
    x, z = v // NZ, lax.rem(v, NZ)

    def at_x(rel):
        return {"vecs": lax.rem(x + rel, NX) * NZ + z}

    turn = 1 - 2 * lax.rem(row, 2)

    def at_z(rel):
        return {"vecs": x * NZ + lax.rem(z + rel, NZ)}

    def local(i):
        if i < 2:
            return pltpu.make_async_copy(
                refl.at[:, :, pl.ds((1 - i) * C, C)], G.at[:, 2 * x + i, z], lsem.at[i]
            )
        half, c = (i - 2) // 2, (i - 2) % 2
        source = vec.at[pl.ds(half * W, W), pl.ds(c * C, C)]
        return pltpu.make_async_copy(source, XB.at[c] if half else RET.at[0, c], lsem.at[i])

    for i in range(6):
        local(i).start()

    barrier = pltpu.get_barrier_semaphore()
    for rel in (1, 2, 3):
        pl.semaphore_signal(barrier, inc=1, device_id=at_x(rel), device_id_type=MESH)
    for rel in range(1, NZ):
        pl.semaphore_signal(barrier, inc=1, device_id=at_z(rel), device_id_type=MESH)
    for rel in (1, ROWS - 1):
        beside = {"rows": lax.rem(row + rel, ROWS)}
        pl.semaphore_signal(barrier, inc=1, device_id=beside, device_id_type=MESH)
    for i in range(6):
        local(i).wait()
    pl.semaphore_wait(barrier, 12)

    def past_x(rel):
        return lax.rem(x + NX - rel, NX)

    def past_z(rel):
        return lax.rem(z + NZ - rel, NZ)

    def remote(slot, u, i, target):
        return pltpu.make_async_remote_copy(
            slot, slot, gs.at[u, i], gr.at[u, i], device_id=target, device_id_type=MESH
        )

    def xshard(u, rel, source):
        return remote(G.at[u, pl.ds(2 * source, 2), z], u, 6 + rel, at_x(rel))

    def zshard(u, rel, source):
        return remote(G.at[u, pl.ds(2 * x, 2), source], u, 5 + rel, at_z(rel))

    def xcolumn(u, i, side, rel, source):
        return remote(G.at[u, 2 * source + side], u, i, at_x(rel))

    def zrow(u, way, k, back):
        step = NZ + (turn if way == 0 else -turn)
        source = lax.rem(z + 5 * NZ - (step - NZ) * back, NZ)
        return remote(G.at[u, pl.ds(1, 7), source], u, k - 1 + 4 * way, at_z(step))

    HOPS = (4, 3)
    SIDES = tuple((side, rel) for rel in (1, 3, 2) for side in (1, 0))

    def unless_zero(side, source, run):
        if side == 1:
            run()
        else:
            pl.when(source != 0)(run)

    def by_row(u, k):
        if k == 0:
            for rel in (1, 3, 2):
                xshard(u, rel, past_x(rel)).wait_recv()
        for way in (0, 1):
            if 1 <= k <= HOPS[way]:
                zrow(u, way, k, k).wait_recv()
            if k < HOPS[way]:
                zrow(u, way, k + 1, k).start()

    def by_column(u, k):
        if k == 0:
            for rel in (1, 7, 2, 6, 3, 5, 4):
                zshard(u, rel, z).start()
        if k == 1:
            for rel in (1, 7, 2, 6, 3, 5, 4):
                zshard(u, rel, past_z(rel)).wait_recv()
            for i, (side, rel) in enumerate(SIDES):
                unless_zero(side, x, lambda: xcolumn(u, i, side, rel, x).start())
        if k == 2:
            for i, (side, rel) in enumerate(SIDES):
                unless_zero(side, past_x(rel), lambda: xcolumn(u, i, side, rel, past_x(rel)).wait_recv())

    def finish_by_row(u):
        for way in (0, 1):
            for k in range(1, HOPS[way] + 1):
                zrow(u, way, k, k - 1).wait_send()
        for rel in (1, 2, 3):
            xshard(u, rel, x).wait_send()

    def finish_by_column(u):
        for rel in range(1, NZ):
            zshard(u, rel, z).wait_send()
        for i, (side, rel) in enumerate(SIDES):
            unless_zero(side, x, lambda: xcolumn(u, i, side, rel, x).wait_send())

    by_column(0, 0)
    for u in (2, 4, 6):
        for rel in (1, 3, 2):
            xshard(u, rel, x).start()
    by_column(1, 0)
    by_column(0, 1)
    by_column(1, 1)
    by_row(2, 0)
    by_column(3, 0)
    by_row(2, 1)
    by_column(0, 2)

    def wave(s, events):
        for run, ahead, k in events:
            pl.when(s + ahead < UNITS)(lambda: run(s + ahead, k))

    AFTER_EVEN = ((by_row, 2, 3), (by_row, 4, 1), (by_column, 3, 1), (by_column, 5, 0), (by_column, 1, 2))
    AFTER_ODD = ((by_row, 3, 2), (by_row, 5, 0), (by_row, 1, 4))

    def prepare(u):
        left = jnp.concatenate([G[u, 2 * i + 1].reshape(C, C) for i in range(NX)], axis=0)
        right = jnp.concatenate(
            [jnp.zeros((C, C), F32)] + [G[u, 2 * i].reshape(C, C) for i in range(1, NX)], axis=0
        )
        vh, vl = split(jnp.concatenate([left, right], axis=1))
        th, tl = vh.T, vl.T
        VH[u], VL[u] = vh, vl
        upper = product((th[:C], tl[:C]), (vh, vl))
        lower = product((th[C:, C:], tl[C:, C:]), (vh[C:, C:], vl[C:, C:]))
        grams = [upper[:, :C], lower]
        inverses = narrow_inverse(grams)
        for half in (16, 32, 64):
            inverses = double(grams, inverses, half)
        (ah, al), (ch, cl) = split(inverses[0]), split(inverses[1])
        corner = product((ah, al), split(product(split(upper[:, C:]), (ch, cl))))
        bh, bl = split(-corner)
        wide = (jnp.concatenate([ah, bh], axis=1), jnp.concatenate([al, bl], axis=1))
        ZH[u, :C], ZL[u, :C] = split(product(wide, (th, tl)))
        ZH[u, C:], ZL[u, C:] = split(product((ch, cl), (th[C:], tl[C:])))

    def up(t, c):
        return pltpu.make_async_remote_copy(
            UPO.at[t, c], BEN.at[t, c], us.at[t, c], ur.at[t, c],
            device_id={"rows": lax.rem(row + ROWS - 1, ROWS)}, device_id_type=MESH,
        )

    def down(t, c):
        return pltpu.make_async_remote_copy(
            DNO.at[t, c], RET.at[t + 1, c], ds.at[t, c], dr.at[t, c],
            device_id={"rows": lax.rem(row + 1, ROWS)}, device_id_type=MESH,
        )

    def solved_of(u, top, bottom):
        (th, tl), (bh, bl) = split(top), split(bottom)
        rh = jnp.concatenate([th, bh], axis=0)
        rl = jnp.concatenate([tl, bl], axis=0)
        wide = dot(ZH[u], jnp.concatenate([rh, rl], axis=1))
        return split(wide[:, :C] + (wide[:, C:] + dot(ZL[u], rh)))

    def change(u, start, solved):
        wide = dot(VH[u, start : start + W], jnp.concatenate(solved, axis=1))
        return wide[:, :C] + (wide[:, C:] + dot(VL[u, start : start + W], solved[0]))

    def even(t):
        u = 2 * t
        for c in range(2):

            @pl.when((row > 0) & (t > 0))
            def _():
                down(t - 1, c).wait_recv()

            top, bottom = RET[t, c], XB[c]
            solved = solved_of(u, top, bottom)
            top = top - change(u, 0, solved)

            @pl.when(row > 0)
            def _():
                UPO[t, c] = top
                up(t, c).start()

            @pl.when(row == 0)
            def _():
                RET[t + 1, c] = top

            XB[c] = bottom - change(u, W, solved)

    def odd(t):
        u = 2 * t + 1
        for c in range(2):

            @pl.when(row < ROWS - 1)
            def _():
                up(t, c).wait_recv()

            top, bottom = XB[c], BEN[t, c]
            solved = solved_of(u, top, bottom)
            bottom = bottom - change(u, W, solved)

            @pl.when(row < ROWS - 1)
            def _():
                DNO[t, c] = bottom
                down(t, c).start()

            @pl.when(row == ROWS - 1)
            def _():
                BEN[t + 1, c] = bottom

            XB[c] = top - change(u, 0, solved)

    @pl.when(row == ROWS - 1)
    def _():
        BEN[0] = jnp.zeros((2, W, C), F32)

    def tick(t, carry):
        pl.when(t > 0)(lambda: even(t - 1))

        @pl.when(t > 0)
        def _():
            wave(2 * t - 2, AFTER_EVEN)
            prepare(2 * t - 1)

        pl.when(t > 0)(lambda: odd(t - 1))

        @pl.when(t < STEPS)
        def _():
            pl.when(t > 0)(lambda: wave(2 * t - 1, AFTER_ODD))
            prepare(2 * t)

        @pl.when(t == 0)
        def _():
            by_row(2, 2)
            by_row(4, 0)

        return carry

    lax.fori_loop(0, STEPS + 1, tick, 0)

    def result(half, c):
        target = out.at[pl.ds(half * W, W), pl.ds(c * C, C)]
        return pltpu.make_async_copy(XB.at[c] if half else RET.at[STEPS, c], target, osem.at[half, c])

    for c in range(2):
        result(1, c).start()
    for c in range(2):

        @pl.when(row > 0)
        def _():
            down(STEPS - 1, c).wait_recv()

        result(0, c).start()

    def finish_pair(t, carry):
        pl.when(t == 0)(lambda: finish_by_column(2 * t))
        pl.when(t != 0)(lambda: finish_by_row(2 * t))
        finish_by_column(2 * t + 1)
        for c in range(2):
            pl.when(row > 0)(lambda: up(t, c).wait_send())
            pl.when(row < ROWS - 1)(lambda: down(t, c).wait_send())
        return carry

    lax.fori_loop(0, STEPS, finish_pair, 0)
    for half in range(2):
        for c in range(2):
            result(half, c).wait()


def local(vectors, reflectors):
    sem = pltpu.SemaphoreType.DMA
    anywhere = pl.BlockSpec(memory_space=pl.ANY)
    return pl.pallas_call(
        kernel,
        out_shape=jax.ShapeDtypeStruct(vectors.shape, F32),
        in_specs=[anywhere, anywhere],
        out_specs=anywhere,
        scratch_shapes=[
            pltpu.VMEM((UNITS, 2 * NX, NZ, 16, C), F32),
            pltpu.VMEM((UNITS, 2 * W, W), BF16),
            pltpu.VMEM((UNITS, 2 * W, W), BF16),
            pltpu.VMEM((UNITS, W, 2 * W), BF16),
            pltpu.VMEM((UNITS, W, 2 * W), BF16),
            pltpu.VMEM((STEPS + 1, 2, W, C), F32),
            pltpu.VMEM((STEPS + 1, 2, W, C), F32),
            pltpu.VMEM((STEPS, 2, W, C), F32),
            pltpu.VMEM((STEPS, 2, W, C), F32),
            pltpu.VMEM((2, W, C), F32),
            sem((6,)),
            sem((2, 2)),
            sem((UNITS, 13)),
            sem((UNITS, 13)),
            sem((STEPS, 2)),
            sem((STEPS, 2)),
            sem((STEPS, 2)),
            sem((STEPS, 2)),
        ],
        compiler_params=pltpu.CompilerParams(
            collective_id=0, has_side_effects=True, vmem_limit_bytes=56 * 2**20
        ),
    )(vectors, reflectors.reshape(UNITS, 16, W))


def solution(mesh):
    placed = (P("rows", "vecs"), P(None, "rows", "vecs", None))
    return jax.shard_map(
        local, mesh=mesh, in_specs=placed, out_specs=P("rows", "vecs"), check_vma=False
    )
```

time: 95.7 us -> 70.1 us (0.73)
  Pallas kernels: 93.7 us -> 68.1 us
    pallas_call x1, Pallas kernels: 93.7 us -> 68.1 us  [local(): pl.pallas_call(kernel, out_shape=jax.ShapeDtypeStruct(vectors.shape, F32)...]
where the time goes in v2:
time: 70.1 us; the launch traced here: 70 us
  Pallas kernels  68.1 us (97%)
  local copies, waits for them, and re-layouts  1.87 us (3%)
    pallas_call x1, Pallas kernels, local(): pl.pallas_call(kernel, out_shape=jax.ShapeDtypeStruct(vectors.shape, F32)...  68.1 us
    unnamed x1, local copies, waits for them, and re-layouts  1.87 us

profile of v2, /device:TPU:16, one launch (start us, length us, event | category | flops | bytes accessed | tf_op | source)
XLA Modules:
  0.0 70.0 jit_solution(3085847439738276371)
XLA Ops:
  0.0 68.1 %shard_map.28 = f32[512,256]{1,0:T(8,128)} custom-call(f32[512,256]{1,0:T(8,128)} %vec.1, f32[8,16,256]{2,1,0:T(8,128)} %bitcast.1), custom_call_target="tpu_custom_call" | custom-call | tf_op jit(solution)/shard_map/pallas_call | solution.py:342
  68.1 1.9 %copy.4 = f32[512,256]{1,0:T(8,128)} copy(f32[512,256]{1,0:T(8,128)} %shard_map.28) | data formatting | bytes 1048576

commit v3 on v2

--- a/solution.py
+++ b/solution.py
@@ -26,43 +26,58 @@
     return dot(a[0], b[0]) + (dot(a[0], b[1]) + dot(a[1], b[0]))
 
 
+def square(a, b):
+    right = jnp.concatenate(
+        [jnp.concatenate([b[0], b[1]], axis=1), jnp.concatenate([b[0], jnp.zeros_like(b[0])], axis=1)], axis=0
+    )
+    both = dot(jnp.concatenate([a[0], a[1]], axis=1), right)
+    return both[:, :C] + both[:, C:]
+
+
+NARROW = 32
+
+
 def narrow_inverse(blocks):
-    i = lax.broadcasted_iota(jnp.int32, (16, C), 0)
-    lane = lax.broadcasted_iota(jnp.int32, (16, C), 1)
-    j = lane % 16
-    columns, accs = [], []
+    i = lax.broadcasted_iota(jnp.int32, (NARROW, C), 0)
+    lane = lax.broadcasted_iota(jnp.int32, (NARROW, C), 1)
+    j = lane % NARROW
+    packs, accs = [], []
     for block in blocks:
-        packed = block[:16]
-        for k in range(1, C // 16):
-            packed = jnp.where(lane // 16 == k, block[16 * k : 16 * k + 16], packed)
-        packed = jnp.where(i < j, packed, jnp.where(i == j, 0.5 * packed, 0.0))
-        columns.append(
-            [jnp.take_along_axis(packed, lane - j + k, axis=1, mode="promise_in_bounds") for k in range(16)]
-        )
+        packed = block[:NARROW]
+        for k in range(1, C // NARROW):
+            packed = jnp.where(lane // NARROW == k, block[NARROW * k : NARROW * (k + 1)], packed)
+        packs.append(jnp.where(i < j, packed, jnp.where(i == j, 0.5 * packed, 0.0)))
         accs.append(jnp.where(i == j, 1.0, 0.0))
-    for k in range(15, -1, -1):
+    for k in range(NARROW - 1, -1, -1):
+        live = 8 * (k // 8 + 1)
         for n in range(len(blocks)):
-            line = accs[n][k : k + 1] * (1.0 / columns[n][k][k : k + 1])
-            accs[n] = jnp.where(i == k, line, accs[n] - columns[n][k] * line)
+            column = jnp.take_along_axis(
+                packs[n][:live], (lane - j + k)[:live], axis=1, mode="promise_in_bounds"
+            )
+            line = accs[n][k : k + 1] * (1.0 / column[k : k + 1])
+            changed = jnp.where(i[:live] == k, line, accs[n][:live] - column * line)
+            accs[n] = jnp.concatenate([changed, accs[n][live:]], axis=0) if live < NARROW else changed
     ri = lax.broadcasted_iota(jnp.int32, (C, C), 0)
     ci = lax.broadcasted_iota(jnp.int32, (C, C), 1)
-    return [jnp.where(ri // 16 == ci // 16, jnp.concatenate([a] * (C // 16), axis=0), 0.0) for a in accs]
-
-
-def double(grams, inverses, half):
+    inside = ri // NARROW == ci // NARROW
+    return [jnp.where(inside, jnp.concatenate([a] * (C // NARROW), axis=0), 0.0) for a in accs]
+
+
+def widen(grams, inverses):
     ri = lax.broadcasted_iota(jnp.int32, (C, C), 0)
     ci = lax.broadcasted_iota(jnp.int32, (C, C), 1)
-    mask = (ri ^ ci >= half) & (ri ^ ci < 2 * half) & (ri < ci)
-    corners = [split(jnp.where(mask, g, 0.0)) for g in grams]
-    pairs = [split(m) for m in inverses]
-    middles = [split(product(b, m)) for b, m in zip(corners, pairs)]
-    return [m - product(p, q) for m, p, q in zip(inverses, pairs, middles)]
+    above = ri // NARROW < ci // NARROW
+    diagonals = [split(m) for m in inverses]
+    nils = [split(square(d, split(jnp.where(above, g, 0.0)))) for d, g in zip(diagonals, grams)]
+    twice = [split(square(n, n)) for n in nils]
+    nears = [m - square(n, d) for m, n, d in zip(inverses, nils, diagonals)]
+    return [p + square(q, split(p)) for p, q in zip(nears, twice)]
 
 
 def kernel(
     vec, refl, out,
     G, VH, VL, ZH, ZL, RET, BEN, UPO, DNO, XB,
-    lsem, osem, gs, gr, us, ur, ds, dr,
+    lsem, osem, fs, fr, gs, gr, us, ur, ds, dr,
 ):
     row = lax.axis_index("rows")
     v = lax.axis_index("vecs")
@@ -170,21 +185,41 @@
         for i, (side, rel) in enumerate(SIDES):
             unless_zero(side, x, lambda: xcolumn(u, i, side, rel, x).wait_send())
 
+    ARRIVAL = (0, 1, 7, 2, 6, 3, 5, 4)
+
+    def crossing(rel, along, source):
+        i = 3 * along + rel - 1
+        slot = G.at[0, pl.ds(2 * source, 2), past_z(along)]
+        return pltpu.make_async_remote_copy(
+            slot, slot, fs.at[i], fr.at[i], device_id=at_x(rel), device_id_type=MESH
+        )
+
+    for rel in (1, 3, 2):
+        xshard(2, rel, x).start()
     by_column(0, 0)
-    for u in (2, 4, 6):
+    for rel in (1, 3, 2):
+        crossing(rel, 0, x).start()
+    by_row(2, 0)
+    for along in ARRIVAL[1:]:
+        zshard(0, along, past_z(along)).wait_recv()
+        for rel in (1, 3, 2):
+            crossing(rel, along, x).start()
+    by_column(1, 0)
+    for u in (4, 6):
         for rel in (1, 3, 2):
             xshard(u, rel, x).start()
-    by_column(1, 0)
-    by_column(0, 1)
+    by_row(2, 1)
+    by_column(3, 0)
+    by_row(2, 2)
+    for along in ARRIVAL:
+        for rel in (1, 3, 2):
+            crossing(rel, along, past_x(rel)).wait_recv()
     by_column(1, 1)
-    by_row(2, 0)
-    by_column(3, 0)
-    by_row(2, 1)
-    by_column(0, 2)
 
     def wave(s, events):
         for run, ahead, k in events:
-            pl.when(s + ahead < UNITS)(lambda: run(s + ahead, k))
+            taken = (s + ahead < UNITS) & (s > 0) if (ahead, k) in ((2, 3),) else s + ahead < UNITS
+            pl.when(taken)(lambda: run(s + ahead, k))
 
     AFTER_EVEN = ((by_row, 2, 3), (by_row, 4, 1), (by_column, 3, 1), (by_column, 5, 0), (by_column, 1, 2))
     AFTER_ODD = ((by_row, 3, 2), (by_row, 5, 0), (by_row, 1, 4))
@@ -198,17 +233,18 @@
         th, tl = vh.T, vl.T
         VH[u], VL[u] = vh, vl
         upper = product((th[:C], tl[:C]), (vh, vl))
-        lower = product((th[C:, C:], tl[C:, C:]), (vh[C:, C:], vl[C:, C:]))
+        both = dot(th[C:, C:], jnp.concatenate([vh[C:, C:], vl[C:, C:]], axis=1))
+        lower = both[:, :C] + (both[:, C:] + dot(tl[C:, C:], vh[C:, C:]))
         grams = [upper[:, :C], lower]
-        inverses = narrow_inverse(grams)
-        for half in (16, 32, 64):
-            inverses = double(grams, inverses, half)
+        inverses = widen(grams, narrow_inverse(grams))
         (ah, al), (ch, cl) = split(inverses[0]), split(inverses[1])
-        corner = product((ah, al), split(product(split(upper[:, C:]), (ch, cl))))
+        corner = square((ah, al), split(square(split(upper[:, C:]), (ch, cl))))
         bh, bl = split(-corner)
         wide = (jnp.concatenate([ah, bh], axis=1), jnp.concatenate([al, bl], axis=1))
         ZH[u, :C], ZL[u, :C] = split(product(wide, (th, tl)))
-        ZH[u, C:], ZL[u, C:] = split(product((ch, cl), (th[C:], tl[C:])))
+        ZH[u, C:], ZL[u, C:] = split(
+            dot(jnp.concatenate([ch, cl], axis=1), jnp.concatenate([th[C:], th[C:]], axis=0)) + dot(ch, tl[C:])
+        )
 
     def up(t, c):
         return pltpu.make_async_remote_copy(
@@ -283,6 +319,19 @@
     def _():
         BEN[0] = jnp.zeros((2, W, C), F32)
 
+    def finish_first():
+        for along in range(NZ):
+            if along:
+                zshard(0, along, z).wait_send()
+            for rel in (1, 2, 3):
+                crossing(rel, along, x).wait_send()
+
+    def finish_gather(t, carry):
+        pl.when(t == 0)(finish_first)
+        pl.when(t != 0)(lambda: finish_by_row(2 * t))
+        finish_by_column(2 * t + 1)
+        return carry
+
     def tick(t, carry):
         pl.when(t > 0)(lambda: even(t - 1))
 
@@ -291,6 +340,10 @@
             wave(2 * t - 2, AFTER_EVEN)
             prepare(2 * t - 1)
 
+        @pl.when(t == STEPS)
+        def _():
+            lax.fori_loop(0, STEPS, finish_gather, 0)
+
         pl.when(t > 0)(lambda: odd(t - 1))
 
         @pl.when(t < STEPS)
@@ -300,7 +353,7 @@
 
         @pl.when(t == 0)
         def _():
-            by_row(2, 2)
+            by_row(2, 3)
             by_row(4, 0)
 
         return carry
@@ -321,16 +374,13 @@
 
         result(0, c).start()
 
-    def finish_pair(t, carry):
-        pl.when(t == 0)(lambda: finish_by_column(2 * t))
-        pl.when(t != 0)(lambda: finish_by_row(2 * t))
-        finish_by_column(2 * t + 1)
+    def finish_exchange(t, carry):
         for c in range(2):
             pl.when(row > 0)(lambda: up(t, c).wait_send())
             pl.when(row < ROWS - 1)(lambda: down(t, c).wait_send())
         return carry
 
-    lax.fori_loop(0, STEPS, finish_pair, 0)
+    lax.fori_loop(0, STEPS, finish_exchange, 0)
     for half in range(2):
         for c in range(2):
             result(half, c).wait()
@@ -357,6 +407,8 @@
             pltpu.VMEM((2, W, C), F32),
             sem((6,)),
             sem((2, 2)),
+            sem((3 * NZ,)),
+            sem((3 * NZ,)),
             sem((UNITS, 13)),
             sem((UNITS, 13)),
             sem((STEPS, 2)),

time: 70.1 us -> 69 us (0.984); the launches traced: 70 us -> 67.9 us
  Pallas kernels: 68.1 us -> 66 us
    pallas_call x1, Pallas kernels: 68.1 us -> 66 us  [local(): pl.pallas_call(kernel, out_shape=jax.ShapeDtypeStruct(vectors.shape, F32)...]
where the time goes in v3:
time: 69 us; the launch traced here: 67.9 us
  Pallas kernels  66 us (96%)
  local copies, waits for them, and re-layouts  1.87 us (3%)
    pallas_call x1, Pallas kernels, local(): pl.pallas_call(kernel, out_shape=jax.ShapeDtypeStruct(vectors.shape, F32)...  66 us
    unnamed x1, local copies, waits for them, and re-layouts  1.87 us

profile of v3, /device:TPU:16, one launch (start us, length us, event | category | flops | bytes accessed | tf_op | source)
XLA Modules:
  0.0 67.9 jit_solution(12020095652233845431)
XLA Ops:
  0.0 66.0 %shard_map.28 = f32[512,256]{1,0:T(8,128)} custom-call(f32[512,256]{1,0:T(8,128)} %vec.1, f32[8,16,256]{2,1,0:T(8,128)} %bitcast.1), custom_call_target="tpu_custom_call" | custom-call | tf_op jit(solution)/shard_map/pallas_call | solution.py:392
  66.0 1.9 %copy.4 = f32[512,256]{1,0:T(8,128)} copy(f32[512,256]{1,0:T(8,128)} %shard_map.28) | data formatting | bytes 1048576

commit v4 on v3

--- a/solution.py
+++ b/solution.py
@@ -76,7 +76,7 @@
 
 def kernel(
     vec, refl, out,
-    G, VH, VL, ZH, ZL, RET, BEN, UPO, DNO, XB,
+    G, VH, VL, ZH, ZL, RET, BEN, UPO, DNO, XB, SB,
     lsem, osem, fs, fr, gs, gr, us, ur, ds, dr,
 ):
     row = lax.axis_index("rows")
@@ -258,12 +258,10 @@
             device_id={"rows": lax.rem(row + 1, ROWS)}, device_id_type=MESH,
         )
 
-    def solved_of(u, top, bottom):
-        (th, tl), (bh, bl) = split(top), split(bottom)
-        rh = jnp.concatenate([th, bh], axis=0)
-        rl = jnp.concatenate([tl, bl], axis=0)
-        wide = dot(ZH[u], jnp.concatenate([rh, rl], axis=1))
-        return split(wide[:, :C] + (wide[:, C:] + dot(ZL[u], rh)))
+    def part(u, start, rows):
+        high, low = split(rows)
+        wide = dot(ZH[u, :, start : start + W], jnp.concatenate([high, low], axis=1))
+        return wide[:, :C] + (wide[:, C:] + dot(ZL[u, :, start : start + W], high))
 
     def change(u, start, solved):
         wide = dot(VH[u, start : start + W], jnp.concatenate(solved, axis=1))
@@ -272,13 +270,16 @@
     def even(t):
         u = 2 * t
         for c in range(2):
+            SB[c] = part(u, W, XB[c])
+
+        for c in range(2):
 
             @pl.when((row > 0) & (t > 0))
             def _():
                 down(t - 1, c).wait_recv()
 
             top, bottom = RET[t, c], XB[c]
-            solved = solved_of(u, top, bottom)
+            solved = split(SB[c] + part(u, 0, top))
             top = top - change(u, 0, solved)
 
             @pl.when(row > 0)
@@ -295,13 +296,16 @@
     def odd(t):
         u = 2 * t + 1
         for c in range(2):
+            SB[c] = part(u, 0, XB[c])
+
+        for c in range(2):
 
             @pl.when(row < ROWS - 1)
             def _():
                 up(t, c).wait_recv()
 
             top, bottom = XB[c], BEN[t, c]
-            solved = solved_of(u, top, bottom)
+            solved = split(SB[c] + part(u, W, bottom))
             bottom = bottom - change(u, W, solved)
 
             @pl.when(row < ROWS - 1)
@@ -405,6 +409,7 @@
             pltpu.VMEM((STEPS, 2, W, C), F32),
             pltpu.VMEM((STEPS, 2, W, C), F32),
             pltpu.VMEM((2, W, C), F32),
+            pltpu.VMEM((2, W, C), F32),
             sem((6,)),
             sem((2, 2)),
             sem((3 * NZ,)),

time: 69 us -> 69.2 us (level)
  no operation moved by 1% of the time
where the time goes in v4:
time: 69.2 us; the launch traced here: 68.2 us
  Pallas kernels  66.3 us (96%)
  local copies, waits for them, and re-layouts  1.87 us (3%)
    pallas_call x1, Pallas kernels, local(): pl.pallas_call(kernel, out_shape=jax.ShapeDtypeStruct(vectors.shape, F32)...  66.3 us
    unnamed x1, local copies, waits for them, and re-layouts  1.87 us

profile of v4, /device:TPU:16, one launch (start us, length us, event | category | flops | bytes accessed | tf_op | source)
XLA Modules:
  0.0 68.2 jit_solution(17114749356837820550)
XLA Ops:
  0.0 66.3 %shard_map.28 = f32[512,256]{1,0:T(8,128)} custom-call(f32[512,256]{1,0:T(8,128)} %vec.1, f32[8,16,256]{2,1,0:T(8,128)} %bitcast.1), custom_call_target="tpu_custom_call" | custom-call | tf_op jit(solution)/shard_map/pallas_call | solution.py:396
  66.3 1.9 %copy.4 = f32[512,256]{1,0:T(8,128)} copy(f32[512,256]{1,0:T(8,128)} %shard_map.28) | data formatting | bytes 1048576

commit v5 on v3

--- a/solution.py
+++ b/solution.py
@@ -238,13 +238,13 @@
         grams = [upper[:, :C], lower]
         inverses = widen(grams, narrow_inverse(grams))
         (ah, al), (ch, cl) = split(inverses[0]), split(inverses[1])
-        corner = square((ah, al), split(square(split(upper[:, C:]), (ch, cl))))
-        bh, bl = split(-corner)
-        wide = (jnp.concatenate([ah, bh], axis=1), jnp.concatenate([al, bl], axis=1))
-        ZH[u, :C], ZL[u, :C] = split(product(wide, (th, tl)))
-        ZH[u, C:], ZL[u, C:] = split(
+        middle = split(square((ah, al), split(upper[:, C:])))
+        zh, zl = split(
             dot(jnp.concatenate([ch, cl], axis=1), jnp.concatenate([th[C:], th[C:]], axis=0)) + dot(ch, tl[C:])
         )
+        ZH[u, C:], ZL[u, C:] = zh, zl
+        head = product((ah, al), (th[:C], tl[:C]))
+        ZH[u, :C], ZL[u, :C] = split(head - product(middle, (zh, zl)))
 
     def up(t, c):
         return pltpu.make_async_remote_copy(

time: 69 us -> 68.7 us (level)
  no operation moved by 1% of the time
where the time goes in v5:
time: 68.7 us; the launch traced here: 68.1 us
  Pallas kernels  66.3 us (97%)
  local copies, waits for them, and re-layouts  1.87 us (3%)
    pallas_call x1, Pallas kernels, local(): pl.pallas_call(kernel, out_shape=jax.ShapeDtypeStruct(vectors.shape, F32)...  66.3 us
    unnamed x1, local copies, waits for them, and re-layouts  1.87 us

profile of v5, /device:TPU:16, one launch (start us, length us, event | category | flops | bytes accessed | tf_op | source)
XLA Modules:
  0.0 68.1 jit_solution(13487308289038355471)
XLA Ops:
  0.0 66.3 %shard_map.28 = f32[512,256]{1,0:T(8,128)} custom-call(f32[512,256]{1,0:T(8,128)} %vec.1, f32[8,16,256]{2,1,0:T(8,128)} %bitcast.1), custom_call_target="tpu_custom_call" | custom-call | tf_op jit(solution)/shard_map/pallas_call | solution.py:392
  66.3 1.9 %copy.4 = f32[512,256]{1,0:T(8,128)} copy(f32[512,256]{1,0:T(8,128)} %shard_map.28) | data formatting | bytes 1048576
